TPU v7x, 512 devices: a whole 4x8x8 slice. The times are simulated.
512 devices in a mesh: scen: 8 (over y), blk: 64 (over z, x, core).
Axes of the slice: x: 4, y: 8, z: 8, core: 2. Of those that a mesh axis runs over, the one named last changes fastest.
Arguments:
- returns: bfloat16 [512, 32768], P(('scen', 'blk')), may hold values from -6 to 6
- vol_hist: float32 [512, 32768], P(('scen', 'blk')), may hold values from 0.5 to 5.5, as said below
- vol_now: float32 [32768], replicated, may hold values from 0.5 to 2
- sensitivity: bfloat16 [16384, 128, 128], P('blk'), may hold values from -0.109375 to 0.109375
- block_pairs: int32 [16384, 3], P('blk'), may hold values from 0 to 255, as said below
- book_order: int32 [128], replicated, may hold values from 0 to 127, each once
Outputs:
- profit_loss: float32 [512, 16384], P('scen', 'blk')
- book_rms: float32 [16384], P('blk')
Inputs may be any that keep to these rules, and one draw needn't show every extreme that they name: `block_pairs`: each index k of blk holds 256 slots; their factor blocks lie in k * 4 to k * 4 + 3; on each index the live slots come first; some index has all 256 slots live. `vol_hist`: positive volatilities.
All inputs are finite; a program needn't handle non-finite values.
Results may differ from a plain program's by a relative error of at most 0.0029.
Values may be sent and summed in bfloat16 or wider, within the bound.
A program may use at most 64 MiB of HBM per device.

v0:
```python
import jax
import jax.numpy as jnp
from jax import lax
from jax.sharding import PartitionSpec as P


def shards(returns, vol_hist, vol_now, sensitivity, block_pairs, book_order):
    rescaled = (returns.astype(jnp.float32) * vol_now[None, :] / vol_hist).astype(jnp.bfloat16)
    groups = lax.axis_size("blk")
    column = lax.axis_index("blk")
    block_size = sensitivity.shape[1]
    own_width = rescaled.shape[1] // groups
    gathered = lax.all_gather(rescaled, "blk", axis=0, tiled=True)
    own_shocks = lax.dynamic_slice_in_dim(gathered, column * own_width, own_width, 1)
    scen_rows = own_shocks.shape[0]
    local_blocks = own_shocks.reshape(scen_rows, own_width // block_size, block_size)
    factor_local = block_pairs[:, 0] - column * (own_width // block_size)
    picked = jnp.take(local_blocks, factor_local, axis=1)
    products = jnp.einsum("skc,kcd->ksd", picked, sensitivity, preferred_element_type=jnp.float32)
    book_blocks = book_order.shape[0]
    matches = book_order[None, :] == block_pairs[:, 1][:, None]
    position = jnp.sum(
        jnp.where(matches, jnp.arange(book_blocks, dtype=jnp.int32)[None, :], 0), axis=1
    )
    live_weight = block_pairs[:, 2].astype(jnp.float32)
    selector = jnp.where(
        jnp.arange(book_blocks, dtype=jnp.int32)[:, None] == position[None, :],
        live_weight[None, :],
        0.0,
    )
    partial_sum = jnp.einsum("bk,ksd->bsd", selector, products, precision=lax.Precision.HIGHEST)
    owned_books = lax.psum_scatter(partial_sum, "blk", scatter_dimension=0, tiled=True)
    profit_loss = owned_books.transpose(1, 0, 2).reshape(scen_rows, -1)
    squares = lax.psum(jnp.sum(profit_loss * profit_loss, axis=0), "scen")
    total_rows = scen_rows * lax.axis_size("scen")
    book_rms = jnp.sqrt(squares / total_rows + 1e-06)
    return (profit_loss, book_rms)


def solution(mesh):
    return jax.shard_map(
        shards,
        mesh=mesh,
        in_specs=(
            P(("scen", "blk"), None),
            P(("scen", "blk"), None),
            P(),
            P("blk", None, None),
            P("blk", None),
            P(),
        ),
        out_specs=(P("scen", "blk"), P("blk")),
        check_vma=False,
    )
```

profile of v0, /device:TPU:2, one launch (start us, length us, event | category | flops | bytes accessed | tf_op | source)
XLA Modules:
  0.0 306.9 jit_solution(5500297832278596794)
XLA Ops:
  7.2 0.0 all-gather.3.cloned.1.call-start
  7.2 1.9 convert_bitcast_fusion
  9.1 0.0 all-gather.3.cloned.1.call-update
  9.1 0.0 reduce-scatter.2.cloned.1.call-start
  9.2 0.7 and_reduce_fusion
  9.9 0.8 fusion.15
  10.7 0.8 select_reduce_fusion
  11.5 93.0 %all-gather.3.cloned.1.call-done = bf16[64,1,32768]{2,1,0:T(2,128)(2,1)} async-done(((bf16[1,1,32768]{2,1,0:T(2,128)(2,1)}), bf16[64,1,32768]{2,1,0:T(2,128)(2,1)}) %all-gather.3.cloned.1.call-update) | async-done | bytes 4194320 | tf_op jit(solution)/shard_map/all_gather | solution.py:13
  104.5 1.3 dynamic-slice_reduce_fusion
  105.8 3.0 gather_fusion
  108.8 7.0 %fusion.2 = f32[256,64,128]{2,1,0:T(8,128)S(1)} fusion(bf16[256,128,128]{2,1,0:T(8,128)(2,1)} %param.9, bf16[256,64,128]{2,1,0:T(8,128)(2,1)} %gather_fusion, pred[256]{0:T(512)(128)(4,1)S(1)} %get-tuple-element.2), kind=kOutput, calls=%fused_computation.3 | convolution fusion | flops 538968064 | bytes 20971776 | tf_op jit(solution)/shard_map/skc,kcd->ksd/dot_general | solution.py:19
  115.9 10.2 %fusion = f32[128,64,128]{2,0,1:T(8,128)S(1)} fusion(f32[256,64,128]{2,1,0:T(8,128)S(1)} %fusion.2, f32[256]{0:T(256)S(1)} %bitcast.32, s32[256]{0:T(256)S(1)} %select_reduce_fusion), kind=kOutput, calls=%fused_computation.1 | convolution fusion | flops 3221291008 | bytes 12584960 | tf_op jit(solution)/shard_map/bk,ksd->bsd/dot_general | solution.py:31
  126.1 4.4 %copy.18 = f32[128,64,128]{2,1,0:T(8,128)} copy(f32[128,64,128]{2,0,1:T(8,128)S(1)} %fusion) | data formatting | bytes 8388608 | tf_op jit(solution)/shard_map/bk,ksd->bsd/dot_general | solution.py:31
  130.4 0.0 reduce-scatter.2.cloned.1.call-update
  130.5 149.7 %reduce-scatter.2.cloned.1.call-done = f32[2,64,128]{2,1,0:T(8,128)} async-done(((f32[128,64,128]{2,1,0:T(8,128)}), f32[2,64,128]{2,1,0:T(8,128)}) %reduce-scatter.2.cloned.1.call-update) | async-done | bytes 65552 | tf_op jit(solution)/shard_map/reduce_scatter | solution.py:32
  280.2 0.9 fusion.9
  281.1 17.0 %psum.7 = f32[256]{0:T(256)S(1)} all-reduce(f32[256]{0:T(256)S(1)} %bitcast.29), channel_id=1, replica_groups=mesh['scen'=8,'blk'=64] {'scen'}, use_global_device_ids=true, to_apply=%region_3.4 | all-reduce | flops 256 | bytes 2048 | tf_op jit(solution)/shard_map/psum | solution.py:34
  298.0 0.6 add_sqrt_fusion
  298.6 1.5 copy_bitcast_fusion
  (2 shorter events, 0.0 us)
Async XLA Ops:
  7.2 97.4 %all-gather.3.cloned.1.call-start = ((), (), s32[]{:S(2)}) async-start(), calls=%async_computation.2 | async-start | bytes 8519680 | tf_op jit(solution)/shard_map/all_gather | solution.py:13
  9.1 271.0 %reduce-scatter.2.cloned.1.call-start = ((), (), s32[]{:S(2)}) async-start(), calls=%async_computation.1 | async-start | bytes 4259840 | tf_op jit(solution)/shard_map/reduce_scatter | solution.py:32
Sparse Core Ops, SparseCore 0:
  11.3 93.1 all-gather.2
  130.6 149.5 reduce-scatter.1
where the time goes:
time: 307 us
  waiting for transfers between devices  243 us (79%)
  matrix products  17.2 us (6%)
  blocking collectives  17 us (6%)
  between operations  14.1 us (5%)
  local copies, waits for them, and re-layouts  10.1 us (3%)
  other arithmetic  5.67 us (2%)
    reduce_scatter x1, waiting for transfers between devices, shards(): lax.psum_scatter(partial_sum, 'blk', scatter_dimension=0, tiled=True)  150 us
    all_gather x1, waiting for transfers between devices, shards(): gathered = lax.all_gather(rescaled, 'blk', axis=0, tiled=True)  93 us
    psum x1, blocking collectives, shards(): squares = lax.psum(jnp.sum(profit_loss * profit_loss, axis=0), 'scen')  17 us
    dot_general x1, matrix products, shards(): jnp.einsum('bk,ksd->bsd', selector, products, precision=lax.Precision.HIG...  10.2 us
    dot_general x1, matrix products, shards(): jnp.einsum('skc,kcd->ksd', picked, sensitivity, preferred_element_type=jn...  7.02 us
  transfers between devices with their start and end apart: 2, of which 2 were waited for; matrix products, arithmetic and copies ran while one was open for 1% of the time, Pallas kernels for 0%

commit v1 on v0

--- a/solution.py
+++ b/solution.py
@@ -10,7 +10,11 @@
     column = lax.axis_index("blk")
     block_size = sensitivity.shape[1]
     own_width = rescaled.shape[1] // groups
-    gathered = lax.all_gather(rescaled, "blk", axis=0, tiled=True)
+    length = lax.axis_size("blk")
+    repeats = [length if d == 0 else 1 for d in range(rescaled.ndim)]
+    gathered = lax.all_to_all(
+        jnp.tile(rescaled, repeats), "blk", split_axis=0, concat_axis=0, tiled=True
+    )
     own_shocks = lax.dynamic_slice_in_dim(gathered, column * own_width, own_width, 1)
     scen_rows = own_shocks.shape[0]
     local_blocks = own_shocks.reshape(scen_rows, own_width // block_size, block_size)

time: 307 us -> 382 us (1.24)
  local copies, waits for them, and re-layouts: 10.1 us -> 43.9 us
  other arithmetic: 5.67 us -> 29.9 us
  starting transfers between devices: 0.08 us -> 14.2 us
    all_to_all x0 -> x1, waiting for transfers between devices: none -> 95.8 us  [shards(): lax.all_to_all(jnp.tile(rescaled, repeats), 'blk', split_axis=0, concat_a...]
    all_gather x1 -> x0, waiting for transfers between devices: 93 us -> none  [shards(): gathered = lax.all_gather(rescaled, 'blk', axis=0, tiled=True)]
    unnamed x0 -> x6, local copies, waits for them, and re-layouts: none -> 27.6 us
    another operation x0 -> x1, other arithmetic: none -> 26.7 us  [shards(): jnp.tile(rescaled, repeats)]
    all_to_all x0 -> x1, starting transfers between devices: none -> 14.2 us  [shards(): lax.all_to_all(jnp.tile(rescaled, repeats), 'blk', split_axis=0, concat_a...]
    another operation x0 -> x2, local copies, waits for them, and re-layouts: none -> 6.13 us  [shards(): jnp.tile(rescaled, repeats)]
  transfers between devices with their start and end apart: 2 -> 2, of which waited for: 2 -> 2; matrix products, arithmetic and copies ran while one was open for 1% -> 0% of each run, Pallas kernels for 0% -> 0%
where the time goes in v1:
time: 382 us; the launch traced here: 381 us
  waiting for transfers between devices  244 us (64%)
  local copies, waits for them, and re-layouts  43.9 us (11%)
  other arithmetic  29.9 us (8%)
  matrix products  17.3 us (5%)
  blocking collectives  16.9 us (4%)
  starting transfers between devices  14.2 us (4%)
  between operations  14.1 us (4%)
    reduce_scatter x1, waiting for transfers between devices, shards(): lax.psum_scatter(partial_sum, 'blk', scatter_dimension=0, tiled=True)  148 us
    all_to_all x1, waiting for transfers between devices, shards(): lax.all_to_all(jnp.tile(rescaled, repeats), 'blk', split_axis=0, concat_a...  95.8 us
    unnamed x6, local copies, waits for them, and re-layouts  27.6 us
    another operation x1, other arithmetic, shards(): jnp.tile(rescaled, repeats)  26.7 us
    psum x1, blocking collectives, shards(): squares = lax.psum(jnp.sum(profit_loss * profit_loss, axis=0), 'scen')  16.9 us
    all_to_all x1, starting transfers between devices, shards(): lax.all_to_all(jnp.tile(rescaled, repeats), 'blk', split_axis=0, concat_a...  14.2 us
    dot_general x1, matrix products, shards(): jnp.einsum('bk,ksd->bsd', selector, products, precision=lax.Precision.HIG...  10.3 us
  transfers between devices with their start and end apart: 2, of which 2 were waited for; matrix products, arithmetic and copies ran while one was open for 0% of the time, Pallas kernels for 0%

profile of v1, /device:TPU:2, one launch (start us, length us, event | category | flops | bytes accessed | tf_op | source)
XLA Modules:
  0.0 380.6 jit_solution(13877792165904643910)
XLA Ops:
  7.2 1.5 convert_reduce_fusion
  8.7 5.6 %tile.2 = bf16[64,1,32768]{2,1,0:T(2,128)(2,1)} broadcast(bf16[32768]{0:T(1024)(128)(2,1)S(1)} %convert_reduce_fusion), dimensions={2} | broadcast | bytes 4259840 | tf_op jit(solution)/shard_map/tile | solution.py:16
  14.3 0.5 broadcast.37
  14.8 26.7 %reduce.7 = bf16[64,32768]{1,0:T(8,128)(2,1)} reduce(bf16[64,1,32768]{2,1,0:T(2,128)(2,1)} %tile.2, bf16[]{:T(256)} %broadcast.37), dimensions={1}, to_apply=%tile.2.reduce_sub_computation | reduce | bytes 8388610 | tf_op jit(solution)/shard_map/tile | solution.py:16
  41.5 7.8 %reshape.48 = bf16[64,2,16384]{2,1,0:T(2,128)(2,1)} reshape(bf16[64,32768]{1,0:T(8,128)(2,1)} %reduce.7) | data formatting | bytes 8388608
  49.3 0.0 copy-start
  49.3 14.2 %all-to-all-start = ((bf16[64,2,16384]{2,1,0:T(2,128)(2,1)}), bf16[64,2,16384]{2,1,0:T(2,128)(2,1)}, u32[]{:S(2)}, u32[]{:S(2)}) async-start(bf16[64,2,16384]{2,1,0:T(2,128)(2,1)} %reshape.48), calls=%async_computation | async-start | bytes 8388608 | tf_op jit(solution)/shard_map/all_to_all | solution.py:15
  63.5 0.0 reduce-scatter.2.cloned.1.call-start
  63.6 0.0 copy-done
  63.6 0.0 copy-done.1
  63.6 0.2 select_reduce_fusion
  63.8 95.8 %all-to-all-done = bf16[64,2,16384]{2,1,0:T(2,128)(2,1)} async-done(((bf16[64,2,16384]{2,1,0:T(2,128)(2,1)}), bf16[64,2,16384]{2,1,0:T(2,128)(2,1)}, u32[]{:S(2)}, u32[]{:S(2)}) %all-to-all-start) | async-done | bytes 4194336 | tf_op jit(solution)/shard_map/all_to_all | solution.py:15
  159.6 19.8 %reshape.49 = bf16[64,1,32768]{2,1,0:T(2,128)(2,1)} reshape(bf16[64,2,16384]{2,1,0:T(2,128)(2,1)} %all-to-all-done) | data formatting | bytes 8388608
  179.4 1.3 dynamic-slice_reduce_fusion
  180.7 3.0 gather_fusion
  183.7 7.0 %fusion.2 = f32[256,64,128]{2,1,0:T(8,128)S(1)} fusion(bf16[256,128,128]{2,1,0:T(8,128)(2,1)} %param.9, bf16[256,64,128]{2,1,0:T(8,128)(2,1)} %gather_fusion, pred[256]{0:T(512)(128)(4,1)S(1)} %get-tuple-element.2), kind=kOutput, calls=%fused_computation.3 | convolution fusion | flops 538968064 | bytes 20971776 | tf_op jit(solution)/shard_map/skc,kcd->ksd/dot_general | solution.py:23
  190.8 10.3 %fusion = f32[128,64,128]{2,0,1:T(8,128)S(1)} fusion(f32[256,64,128]{2,1,0:T(8,128)S(1)} %fusion.2, f32[256]{0:T(256)S(1)} %bitcast.30, s32[256]{0:T(256)S(1)} %select_reduce_fusion), kind=kOutput, calls=%fused_computation.1 | convolution fusion | flops 3221291008 | bytes 12584960 | tf_op jit(solution)/shard_map/bk,ksd->bsd/dot_general | solution.py:35
  201.0 4.4 %copy.18 = f32[128,64,128]{2,1,0:T(8,128)} copy(f32[128,64,128]{2,0,1:T(8,128)S(1)} %fusion) | data formatting | bytes 8388608 | tf_op jit(solution)/shard_map/bk,ksd->bsd/dot_general | solution.py:35
  205.4 0.0 reduce-scatter.2.cloned.1.call-update
  205.4 148.5 %reduce-scatter.2.cloned.1.call-done = f32[2,64,128]{2,1,0:T(8,128)} async-done(((f32[128,64,128]{2,1,0:T(8,128)}), f32[2,64,128]{2,1,0:T(8,128)}) %reduce-scatter.2.cloned.1.call-update) | async-done | bytes 65552 | tf_op jit(solution)/shard_map/reduce_scatter | solution.py:36
  353.9 0.9 fusion.9
  354.8 16.9 %psum.7 = f32[256]{0:T(256)S(1)} all-reduce(f32[256]{0:T(256)S(1)} %bitcast.27), channel_id=1, replica_groups=mesh['scen'=8,'blk'=64] {'scen'}, use_global_device_ids=true, to_apply=%region_3.4 | all-reduce | flops 256 | bytes 2048 | tf_op jit(solution)/shard_map/psum | solution.py:38
  371.7 0.6 add_sqrt_fusion
  372.2 1.5 copy_bitcast_fusion
  (5 shorter events, 0.1 us)
Async XLA Ops:
  49.3 14.3 %copy-start = (s32[256,3]{0,1:T(4,128)S(1)}, s32[256,3]{0,1:T(4,128)}, u32[]{:S(2)}) copy-start(s32[256,3]{0,1:T(4,128)} %param.10) | copy-start | bytes 9220
  49.3 14.3 %copy-start.1 = (s32[128]{0:T(128)S(1)}, s32[128]{0:T(128)}, u32[]{:S(2)}) copy-start(s32[128]{0:T(128)} %param.11) | copy-start | bytes 1540
  49.3 110.3 %all-to-all-start = ((bf16[64,2,16384]{2,1,0:T(2,128)(2,1)}), bf16[64,2,16384]{2,1,0:T(2,128)(2,1)}, u32[]{:S(2)}, u32[]{:S(2)}) async-start(bf16[64,2,16384]{2,1,0:T(2,128)(2,1)} %reshape.48), calls=%async_computation | async-start | bytes 8388608 | tf_op jit(solution)/shard_map/all_to_all | solution.py:15
  63.5 290.4 %reduce-scatter.2.cloned.1.call-start = ((), (), s32[]{:S(2)}) async-start(), calls=%async_computation.2 | async-start | bytes 4259840 | tf_op jit(solution)/shard_map/reduce_scatter | solution.py:36
Sparse Core Ops, SparseCore 0:
  205.5 148.3 reduce-scatter.1
